TPU v7x, 128 devices: a whole 4x4x4 slice. The times are simulated.
128 devices in a mesh: aa: 16 (over y, x), ba: 8 (over z, core).
Axes of the slice: x: 4, y: 4, z: 4, core: 2. Of those that a mesh axis runs over, the one named last changes fastest.
Arguments:
- queries: bfloat16 [8, 128, 8192], P('ba', None, 'aa'), may hold values from -10 to 10
- new_kv: bfloat16 [8, 128, 2, 512], P('ba', 'aa'), may hold values from -4 to 4
- pool: bfloat16 [8, 192, 32, 2, 512], P('ba', 'aa'), may hold values from -4 to 4
- page_table: int32 [8, 64], P('ba', 'aa'), may hold values from 0 to 11, as said below
- ctx_len: int32 [8, 16], P('ba', 'aa'), may hold values from 1 to 128, as said below
- move_page: int32 [8, 112], P('ba', 'aa'), may hold values from 0 to 11, as said below
- move_dest: int32 [8, 112], P('ba', 'aa'), may hold values from 0 to 7, as said below
- append_page: int32 [8, 16], P('ba', 'aa'), may hold values from 0 to 11
Outputs:
- attended: bfloat16 [8, 128, 8192], P('ba', None, 'aa')
- pool_out: bfloat16 [8, 192, 32, 2, 512], P('ba', 'aa')
Inputs may be any that keep to these rules, and one draw needn't show every extreme that they name: `page_table`: the entries of one device are distinct pages of its pool and differ from its leaving pages and its append page. `ctx_len`: for each instance some index of aa holds exactly 128 live rows. `move_page`: the 7 entries of one device are distinct pages of its pool. `move_dest`: A device never names its own instance and names any one instance at most 2 times; for each index of aa one instance is named exactly 2 times by the device of every other instance.
All inputs are finite; a program needn't handle non-finite values.
Results may differ from a plain program's by a relative error of at most 0.0017.
Values may be sent and summed in bfloat16 or wider, within the bound.
No kernel may reach another device: no remote copies, remote signals or barrier semaphores. Data moves between devices by JAX's collectives and lax.ppermute only.
A program may use at most 64 MiB of HBM per device.

v0:
```python
import math
import jax
import jax.numpy as jnp
from jax import lax
from jax.sharding import PartitionSpec as P

HEAD_DIM = 128
MOST = 2
NEG_LARGE = -1e30


def in_one_piece(arrays, axis, split_dim, concat_dim, along):
    widths = [math.prod(a.shape[along:]) for a in arrays]
    both = jnp.concatenate(
        [a.reshape(*a.shape[:along], w) for a, w in zip(arrays, widths)], axis=along
    )
    filled = lax.all_to_all(both, axis, split_axis=split_dim, concat_axis=concat_dim, tiled=True)
    blocks = jnp.split(filled, [sum(widths[:k]) for k in range(1, len(widths))], axis=along)
    return tuple(
        (b.reshape(*filled.shape[:along], *a.shape[along:]) for a, b in zip(arrays, blocks))
    )


def from_everyone(value, axis):
    length = lax.axis_size(axis)
    return lax.all_to_all(
        jnp.broadcast_to(value[None], (length, *value.shape)), axis, 0, 0, tiled=True
    )


def taken_together(value, axis):
    return from_everyone(value, axis).max(axis=0)


def split_up(value, dim, length):
    lengths = value.shape
    blocks = value.reshape(*lengths[:dim], length, lengths[dim] // length, *lengths[dim + 1 :])
    return jnp.moveaxis(blocks, dim, 0)


def sum_at_owner(value, axis, dim):
    length = lax.axis_size(axis)
    blocks = lax.all_to_all(split_up(value, dim, length), axis, 0, 0, tiled=True)
    return jnp.sum(blocks, axis=0)


def in_one_piece_2(arrays, axis, dim, along):
    widths = [math.prod(a.shape[along:]) for a in arrays]
    both = jnp.concatenate(
        [a.reshape(*a.shape[:along], w) for a, w in zip(arrays, widths)], axis=along
    )
    filled = sum_at_owner(both, axis, dim)
    blocks = jnp.split(filled, [sum(widths[:k]) for k in range(1, len(widths))], axis=along)
    return tuple(
        (b.reshape(*filled.shape[:along], *a.shape[along:]) for a, b in zip(arrays, blocks))
    )


def block_plan(total_rows):
    counted = max(1, total_rows // 512)
    length = -(-total_rows // counted)
    length = -(-length // 8) * 8
    return (counted, length)


def combine_parts(former, latter):
    former_max, former_sum, former_out = former
    latter_max, latter_sum, latter_out = latter
    joint_max = jnp.maximum(former_max, latter_max)
    former_scale = jnp.exp(former_max - joint_max)
    latter_scale = jnp.exp(latter_max - joint_max)
    joint_sum = former_sum * former_scale + latter_sum * latter_scale
    joint_out = former_out * former_scale[..., None] + latter_out * latter_scale[..., None]
    return (joint_max, joint_sum, joint_out)


def attend_rows(query_heads, key_rows, visible):
    total_rows = key_rows.shape[0]
    counted, length = block_plan(total_rows)
    query_count, kv_heads, group_size, head_dim = query_heads.shape
    blocked_keys = key_rows.reshape(counted, length, 2, kv_heads, head_dim)
    blocked_mask = visible.reshape(query_count, counted, length).transpose(1, 0, 2)
    scale = 1.0 / math.sqrt(head_dim)

    def block_step(state_now, inputs):
        run_max, run_sum, run_out = state_now
        block_keys, block_mask = inputs
        scores = (
            jnp.einsum(
                "qkgd,rkd->qkgr", query_heads, block_keys[:, 0], preferred_element_type=jnp.float32
            )
            * scale
        )
        allowed = block_mask[:, None, None, :]
        scores = jnp.where(allowed, scores, NEG_LARGE)
        new_max = jnp.maximum(run_max, jnp.max(scores, axis=-1))
        weights = jnp.where(allowed, jnp.exp(scores - new_max[..., None]), 0.0)
        shrink = jnp.exp(run_max - new_max)
        new_sum = run_sum * shrink + jnp.sum(weights, axis=-1)
        block_values = block_keys[:, 1].astype(jnp.float32)
        new_out = run_out * shrink[..., None] + jnp.einsum(
            "qkgr,rkd->qkgd", weights, block_values, precision=lax.Precision.HIGHEST
        )
        return ((new_max, new_sum, new_out), None)

    start_state = (
        jnp.full((query_count, kv_heads, group_size), NEG_LARGE, jnp.float32),
        jnp.zeros((query_count, kv_heads, group_size), jnp.float32),
        jnp.zeros((query_count, kv_heads, group_size, head_dim), jnp.float32),
    )
    finished, _ = lax.scan(block_step, start_state, (blocked_keys, blocked_mask))
    return finished


def local(queries, new_kv, pool, page_table, ctx_len, move_page, move_dest, append_page):
    instances = lax.axis_size("ba")
    position = lax.axis_index("aa")
    pool_pages = pool[0]
    page_rows = pool_pages.shape[1]
    kv_width = pool_pages.shape[-1]
    kv_heads = kv_width // HEAD_DIM
    gathered = lax.all_gather(queries[0], "aa", axis=1, tiled=True)
    query_count = gathered.shape[0]
    query_heads = gathered.reshape(query_count, kv_heads, -1, HEAD_DIM)
    moved_ids = move_page[0]
    targets = move_dest[0]
    move_count = moved_ids.shape[0]
    counter = jnp.arange(move_count, dtype=jnp.int32)
    earlier = (counter[None, :] < counter[:, None]) & (targets[None, :] == targets[:, None])
    slot_index = targets * MOST + jnp.sum(earlier, axis=1)
    select = (jnp.arange(instances * MOST, dtype=jnp.int32)[:, None] == slot_index[None, :]).astype(
        jnp.bfloat16
    )
    picked = jnp.take(pool_pages, moved_ids, axis=0).reshape(move_count, -1)
    outgoing = jnp.dot(select, picked, preferred_element_type=jnp.float32).astype(jnp.bfloat16)
    outgoing = outgoing.reshape(instances, MOST, page_rows, 2, kv_width)
    occupied = (
        jnp.sum(select.astype(jnp.float32), axis=1).astype(jnp.bfloat16).reshape(instances, MOST)
    )
    incoming, arrived = in_one_piece((outgoing, occupied), "ba", 0, 0, 2)
    moved_rows = incoming.reshape(-1, 2, kv_width)
    moved_live = jnp.broadcast_to(
        (arrived > 0.5)[:, :, None], (instances, MOST, page_rows)
    ).reshape(-1)
    resident = jnp.take(pool_pages, page_table[0], axis=0).reshape(-1, 2, kv_width)
    resident_live = jnp.arange(resident.shape[0], dtype=jnp.int32) < ctx_len[0, 0]
    fresh_rows = new_kv[0]
    fresh_count = fresh_rows.shape[0]
    fresh_place = position * fresh_count + jnp.arange(fresh_count, dtype=jnp.int32)
    fresh_visible = fresh_place[None, :] <= jnp.arange(query_count, dtype=jnp.int32)[:, None]
    resident_visible = jnp.broadcast_to(
        resident_live[None, :], (query_count, resident_live.shape[0])
    )
    moved_visible = jnp.broadcast_to(moved_live[None, :], (query_count, moved_live.shape[0]))
    local_part = attend_rows(
        query_heads,
        jnp.concatenate([resident, fresh_rows], axis=0),
        jnp.concatenate([resident_visible, fresh_visible], axis=1),
    )
    moved_part = attend_rows(query_heads, moved_rows, moved_visible)
    partials = combine_parts(local_part, moved_part)
    run_max, run_sum, run_out = partials
    top_max = taken_together(run_max, "aa")
    rescale = jnp.exp(run_max - top_max)
    numerator = (run_out * rescale[..., None]).reshape(query_count, -1, HEAD_DIM)
    denominator = (run_sum * rescale).reshape(query_count, -1)
    numerator, denominator = in_one_piece_2((numerator, denominator), "aa", 1, 2)
    result = numerator / denominator[..., None]
    attended = result.reshape(1, query_count, -1).astype(jnp.bfloat16)
    zero = jnp.zeros((), jnp.int32)
    updated = lax.dynamic_update_slice(
        pool_pages, fresh_rows[None], (append_page[0, 0], zero, zero, zero)
    )
    return (attended, updated[None])


def solution(mesh):
    return jax.shard_map(
        local,
        mesh=mesh,
        in_specs=(
            P("ba", None, "aa"),
            P("ba", "aa", None, None),
            P("ba", "aa", None, None, None),
            P("ba", "aa"),
            P("ba", "aa"),
            P("ba", "aa"),
            P("ba", "aa"),
            P("ba", "aa"),
        ),
        out_specs=(P("ba", None, "aa"), P("ba", "aa", None, None, None)),
        check_vma=False,
    )
```

profile of v0, /device:TPU:0, one launch (start us, length us, event | category | flops | bytes accessed | tf_op | source)
XLA Modules:
  0.0 190.3 jit_solution(174172654630481055)
XLA Ops:
  7.2 0.0 all-gather.3.cloned.1.call-start
  7.2 1.1 copy.173
  8.3 1.7 copy.132
  10.0 0.0 all-gather.3.cloned.1.call-update
  10.0 0.7 fusion.45
  10.7 0.7 compare_and_fusion
  11.4 0.9 convert_reduce_fusion
  12.3 0.7 fusion.46
  12.9 0.1 fusion.42
  13.0 0.1 reshape_reshape.9
  13.1 1.5 gather_fusion.1
  14.6 0.0 copy-start.4
  14.6 0.0 copy-start.3
  14.6 0.3 gather.15
  14.9 0.6 convolution_convert_fusion
  15.5 0.7 reshape_reshape.7
  16.2 1.9 %pad_maximum_fusion = bf16[8,2,32769]{2,1,0:T(2,128)(2,1)} fusion(bf16[8,2,1]{2,1,0:T(2,128)(2,1)S(1)} %reshape_reshape.9, bf16[8,2,32768]{2,1,0:T(2,128)(2,1)S(1)} %reshape_reshape.7), kind=kLoop, calls=%fused_computation.33 | loop fusion | flops 2097216 | bytes 2097216 | tf_op jit(solution)/shard_map/concatenate | solution.py:14
  18.2 5.4 %all-to-all-start = ((bf16[8,2,32769]{2,1,0:T(2,128)(2,1)}), bf16[8,2,32769]{2,1,0:T(2,128)(2,1)S(1)}, u32[]{:S(2)}, u32[]{:S(2)}) async-start(bf16[8,2,32769]{2,1,0:T(2,128)(2,1)} %pad_maximum_fusion), calls=%async_computation | async-start | bytes 2105344 | tf_op jit(solution)/shard_map/all_to_all | solution.py:17
  23.6 0.0 copy-done.4
  24.3 0.1 broadcast_in_dim.123
  24.4 0.1 broadcast_in_dim.124
  24.4 0.0 copy-done.3
  24.5 1.1 gather_fusion
  25.6 0.2 reshape.297
  25.8 0.1 iota_compare_fusion.3
  25.8 0.1 pad_add_fusion
  25.9 0.1 copy_select_fusion
  26.0 13.6 %all-to-all-done = bf16[8,2,32769]{2,1,0:T(2,128)(2,1)S(1)} async-done(((bf16[8,2,32769]{2,1,0:T(2,128)(2,1)}), bf16[8,2,32769]{2,1,0:T(2,128)(2,1)S(1)}, u32[]{:S(2)}, u32[]{:S(2)}) %all-to-all-start) | async-done | bytes 1048640 | tf_op jit(solution)/shard_map/all_to_all | solution.py:17
  39.6 0.1 copy.156
  39.7 0.7 split.17
  40.4 0.8 squeeze.63
  41.3 0.4 fusion.58
  41.6 1.1 copy.158
  42.8 0.1 copy.136
  42.9 0.1 broadcast_in_dim.132
  42.9 0.1 broadcast_in_dim.133
  43.0 15.0 %all-gather.3.cloned.1.call-done = bf16[1,128,8192]{1,2,0:T(8,128)(2,1)} async-done(((bf16[1,128,512]{1,2,0:T(8,128)(2,1)}), bf16[1,128,8192]{1,2,0:T(8,128)(2,1)}) %all-gather.3.cloned.1.call-update) | async-done | bytes 2097168 | tf_op jit(solution)/shard_map/all_gather | solution.py:122
  58.0 0.0 copy-start
  58.1 8.9 %bitcast_reduce_fusion = (f32[128,4,16]{0,2,1:T(8,128)S(1)}, f32[4,512,128,16]{2,1,3,0:T(8,128)}) fusion(pred[512]{0:T(512)(128)(4,1)S(1)} %broadcast_in_dim.133, bf16[128,4,16,128]{0,3,2,1:T(8,128)(2,1)} %bitcast.111, bf16[512,1,4,128]{3,2,1,0:T(4,128)(2,1)S(1)} %get-tuple-element.59), kind=kOutput, calls=%fused_computation.4 | convolution fusion | flops 1086316544 | bytes 19431936 | tf_op jit(solution)/shard_map/while/body/eval_jaxpr/qkgd,rkd->qkgr/dot_general | solution.py:89
  66.9 0.0 copy-done
  66.9 2.9 %fusion.15 = (f32[128,4,16]{0,2,1:T(8,128)S(1)}, f32[4,136,128,16]{2,1,3,0:T(8,128)}) fusion(pred[128,136]{0,1:T(8,128)(4,1)S(1)} %pad_add_fusion, bf16[128,4,16,128]{0,3,2,1:T(8,128)(2,1)S(1)} %bitcast.112, bf16[128,2,4,128]{3,0,2,1:T(8,128)(2,1)S(1)} %copy_select_fusion, bf16[8,2,4,128]{3,0,2,1:T(8,128)(2,1)S(1)} %copy.131), kind=kOutput, calls=%fused_computation.25 | convolution fusion | flops 288825344 | bytes 6882304 | tf_op jit(solution)/shard_map/while/body/eval_jaxpr/qkgd,rkd->qkgr/dot_general | solution.py:89
  69.8 0.8 broadcast_in_dim.138
  70.7 0.0 slice-start
  70.7 5.1 %all-to-all-start.1 = ((f32[16,128,4,16]{1,3,2,0:T(8,128)}), f32[16,128,4,16]{1,3,2,0:T(8,128)S(1)}, u32[]{:S(2)}, u32[]{:S(2)}) async-start(f32[16,128,4,16]{1,3,2,0:T(8,128)} %broadcast_in_dim.138), calls=%async_computation.1 | async-start | bytes 1048576 | tf_op jit(solution)/shard_map/all_to_all | solution.py:26
  75.8 0.0 slice-start.1
  75.8 8.5 %fusion.2 = f32[128,4,16]{0,2,1:T(8,128)S(1)} fusion(f32[4,512,128,16]{2,1,3,0:T(8,128)} %get-tuple-element.69, f32[128,4,16]{0,2,1:T(8,128)S(1)} %get-tuple-element.62, pred[512]{0:T(512)(128)(4,1)S(1)} %broadcast_in_dim.133), kind=kLoop, calls=%fused_computation.8 | loop fusion | flops 20963328 | bytes 16843264 | tf_op jit(solution)/shard_map/while/body/eval_jaxpr/reduce_sum | solution.py:99
  84.3 0.0 slice-done
  84.3 0.0 slice-done.1
  84.3 1.3 fusion.16
  85.6 0.0 copy-start.2
  85.7 5.3 %fusion.17 = f32[4,128,128,16]{2,1,3,0:T(8,128)} fusion(f32[4,136,128,16]{2,1,3,0:T(8,128)S(1)} %bitcast.110, f32[128,4,16]{0,2,1:T(8,128)S(1)} %get-tuple-element.65, pred[128,136]{0,1:T(8,128)(4,1)S(1)} %pad_add_fusion, bf16[8,2,4,128]{3,0,2,1:T(8,128)(2,1)S(1)} %copy.131, bf16[128,2,4,128]{3,0,2,1:T(8,128)(2,1)S(1)} %copy_select_fusion), kind=kOutput, calls=%fused_computation.27 | convolution fusion | flops 1716011008 | bytes 8979456 | tf_op jit(solution)/shard_map/while/body/eval_jaxpr/qkgr,rkd->qkgd/dot_general | solution.py:101
  90.9 0.0 all-to-all-done.1
  91.0 0.0 copy-done.2
  91.0 15.8 %fusion.13 = f32[128,4,16,128]{0,3,2,1:T(8,128)S(1)} fusion(f32[4,128,128,16]{2,1,3,0:T(8,128)} %fusion.17, f32[4,512,128,16]{2,1,3,0:T(8,128)} %get-tuple-element.69, f32[128,4,16]{0,2,1:T(8,128)S(1)} %get-tuple-element.62, pred[512]{0:T(512)(128)(4,1)S(1)} %broadcast_in_dim.133, f32[128,4,16]{0,2,1:T(8,128)S(1)} %get-tuple-element.64, ...), kind=kOutput, calls=%fused_computation.22 | convolution fusion | flops 6465519616 | bytes 25887232 | tf_op jit(solution)/shard_map/while/body/eval_jaxpr/qkgr,rkd->qkgd/dot_general | solution.py:101
  106.8 2.8 %copy.141 = f32[128,16,4,128]{0,2,3,1:T(4,128)S(1)} copy(f32[128,16,4,128]{0,3,2,1:T(8,128)S(1)} %bitcast.113) | data formatting | bytes 8388608 | tf_op jit(solution)/shard_map/concatenate | solution.py:49
  109.6 0.1 exponential_multiply_fusion
  109.6 3.0 %maximum_bitcast_fusion = f32[16,128,4,129]{1,2,3,0:T(4,128)} fusion(f32[128,16,4,1]{0,2,3,1:T(4,128)S(1)} %exponential_multiply_fusion, f32[128,16,4,128]{0,2,3,1:T(4,128)S(1)} %copy.141), kind=kLoop, calls=%fused_computation.18 | loop fusion | flops 1056768 | bytes 8454144 | tf_op jit(solution)/shard_map/transpose | solution.py:38
  112.6 7.3 %all-to-all-start.2 = ((f32[16,128,4,129]{1,2,3,0:T(4,128)}), f32[16,128,4,129]{1,2,3,0:T(4,128)}, u32[]{:S(2)}, u32[]{:S(2)}) async-start(f32[16,128,4,129]{1,2,3,0:T(4,128)} %maximum_bitcast_fusion), calls=%async_computation.2 | async-start | bytes 8454144 | tf_op jit(solution)/shard_map/all_to_all | solution.py:43
  120.5 0.0 copy-start.1
  120.5 59.2 %all-to-all-done.2 = f32[16,128,4,129]{1,2,3,0:T(4,128)} async-done(((f32[16,128,4,129]{1,2,3,0:T(4,128)}), f32[16,128,4,129]{1,2,3,0:T(4,128)}, u32[]{:S(2)}, u32[]{:S(2)}) %all-to-all-start.2) | async-done | bytes 4227104 | tf_op jit(solution)/shard_map/all_to_all | solution.py:43
  179.7 2.9 %reduce_sum.63 = f32[128,4,129]{0,1,2:T(4,128)S(1)} reduce(f32[16,128,4,129]{1,2,3,0:T(4,128)} %all-to-all-done.2, f32[]{:T(128)} %constant.52.clone.1), dimensions={0}, to_apply=%region_7.8 | reduce | flops 990720 | bytes 4491268 | tf_op jit(solution)/shard_map/reduce_sum | solution.py:44
  182.6 0.8 copy.143
  183.4 0.0 copy-done.1
  (19 shorter events, 0.2 us)
Async XLA Ops:
  7.2 50.9 %all-gather.3.cloned.1.call-start = ((), (), s32[]{:S(2)}) async-start(), calls=%async_computation.3 | async-start | bytes 2228224 | tf_op jit(solution)/shard_map/all_gather | solution.py:122
  14.6 9.0 %copy-start.4 = (s32[1,4]{1,0:T(1,128)S(1)}, s32[1,4]{1,0:T(1,128)}, u32[]{:S(2)}) copy-start(s32[1,4]{1,0:T(1,128)} %param.11) | copy-start | bytes 52
  14.6 9.8 %copy-start.3 = (bf16[1,8,2,512]{3,2,1,0:T(2,128)(2,1)S(1)}, bf16[1,8,2,512]{3,2,1,0:T(2,128)(2,1)}, u32[]{:S(2)}) copy-start(bf16[1,8,2,512]{3,2,1,0:T(2,128)(2,1)} %param.9) | copy-start | bytes 49156
  18.2 21.4 %all-to-all-start = ((bf16[8,2,32769]{2,1,0:T(2,128)(2,1)}), bf16[8,2,32769]{2,1,0:T(2,128)(2,1)S(1)}, u32[]{:S(2)}, u32[]{:S(2)}) async-start(bf16[8,2,32769]{2,1,0:T(2,128)(2,1)} %pad_maximum_fusion), calls=%async_computation | async-start | bytes 2105344 | tf_op jit(solution)/shard_map/all_to_all | solution.py:17
  58.0 8.9 %copy-start = (bf16[1,128,8192]{1,2,0:T(8,128)(2,1)S(1)}, bf16[1,128,8192]{1,2,0:T(8,128)(2,1)}, u32[]{:S(2)}) copy-start(bf16[1,128,8192]{1,2,0:T(8,128)(2,1)} %all-gather.3.cloned.1.call-done) | copy-start | bytes 6291460
  70.7 13.6 %slice-start = ((s8[4456448]{0:T(1024)(128)(4,1)}), s8[262144]{0:T(1024)(128)(4,1)S(1)}, s32[]{:S(2)}) async-start(s8[4456448]{0:T(1024)(128)(4,1)} %bitcast.109), calls=%async_computation.4 | async-start | bytes 524288
  70.7 20.2 %all-to-all-start.1 = ((f32[16,128,4,16]{1,3,2,0:T(8,128)}), f32[16,128,4,16]{1,3,2,0:T(8,128)S(1)}, u32[]{:S(2)}, u32[]{:S(2)}) async-start(f32[16,128,4,16]{1,3,2,0:T(8,128)} %broadcast_in_dim.138), calls=%async_computation.1 | async-start | bytes 1048576 | tf_op jit(solution)/shard_map/all_to_all | solution.py:26
  75.8 8.6 %slice-start.1 = ((s8[4456448]{0:T(1024)(128)(4,1)}), s8[4194304]{0:T(1024)(128)(4,1)S(1)}, s32[]{:S(2)}) async-start(s8[4456448]{0:T(1024)(128)(4,1)} %bitcast.109), calls=%async_computation.5 | async-start | bytes 8388608
  85.6 5.3 %copy-start.2 = (bf16[512,1,4,128]{0,3,2,1:T(8,128)(2,1)S(1)}, bf16[512,1,4,128]{0,3,2,1:T(8,128)(2,1)}, u32[]{:S(2)}) copy-start(bf16[512,1,4,128]{0,3,2,1:T(8,128)(2,1)} %copy.158) | copy-start | bytes 1572868
  112.6 67.1 %all-to-all-start.2 = ((f32[16,128,4,129]{1,2,3,0:T(4,128)}), f32[16,128,4,129]{1,2,3,0:T(4,128)}, u32[]{:S(2)}, u32[]{:S(2)}) async-start(f32[16,128,4,129]{1,2,3,0:T(4,128)} %maximum_bitcast_fusion), calls=%async_computation.2 | async-start | bytes 8454144 | tf_op jit(solution)/shard_map/all_to_all | solution.py:43
  120.5 62.9 %copy-start.1 = (bf16[1,12,32,2,512]{4,3,2,1,0:T(2,128)(2,1)}, bf16[1,12,32,2,512]{4,3,2,1,0:T(2,128)(2,1)S(1)}, u32[]{:S(2)}) copy-start(bf16[1,12,32,2,512]{4,3,2,1,0:T(2,128)(2,1)S(1)} %bitcast_dynamic-update-slice_fusion) | copy-start | bytes 2359300
Sparse Core Ops, SparseCore 0:
  10.7 47.2 all-gather.2
where the time goes:
time: 191 us; the launch traced here: 190 us
  waiting for transfers between devices  87.8 us (46%)
  matrix products  33.4 us (17%)
  other arithmetic  21 us (11%)
  starting transfers between devices  17.8 us (9%)
  between operations  15.6 us (8%)
  local copies, waits for them, and re-layouts  14.7 us (8%)
    all_to_all x1, waiting for transfers between devices, sum_at_owner(): lax.all_to_all(split_up(value, dim, length), axis, 0, 0, tiled=True)  59.2 us
    dot_general x2, matrix products, block_step(): jnp.einsum('qkgr,rkd->qkgd', weights, block_values, precision=lax.Precisi...  21 us
    all_gather x1, waiting for transfers between devices, local(): gathered = lax.all_gather(queries[0], 'aa', axis=1, tiled=True)  15 us
    all_to_all x1, waiting for transfers between devices, in_one_piece(): lax.all_to_all(both, axis, split_axis=split_dim, concat_axis=concat_dim,...  13.6 us
    dot_general x2, matrix products, block_step(): jnp.einsum('qkgd,rkd->qkgr', query_heads, block_keys[:, 0], preferred_ele...  11.8 us
    reduce_sum x2, other arithmetic, block_step(): new_sum = run_sum * shrink + jnp.sum(weights, axis=-1)  9.83 us
    all_to_all x1, starting transfers between devices, sum_at_owner(): lax.all_to_all(split_up(value, dim, length), axis, 0, 0, tiled=True)  7.25 us
    all_to_all x1, starting transfers between devices, in_one_piece(): lax.all_to_all(both, axis, split_axis=split_dim, concat_axis=concat_dim,...  5.39 us
  transfers between devices with their start and end apart: 4, of which 3 were waited for; matrix products, arithmetic and copies ran while one was open for 15% of the time, Pallas kernels for 0%

commit v1 on v0

--- a/solution.py
+++ b/solution.py
@@ -119,7 +119,23 @@
     page_rows = pool_pages.shape[1]
     kv_width = pool_pages.shape[-1]
     kv_heads = kv_width // HEAD_DIM
-    gathered = lax.all_gather(queries[0], "aa", axis=1, tiled=True)
+
+    def guide_the_row(local_values):
+        group_axis = "aa"
+        how_many = lax.axis_size(group_axis)
+        so_far_all = [local_values]
+        for pp in range(how_many - 1):
+            main = lax.ppermute(
+                so_far_all[-1],
+                group_axis,
+                perm=[(hop_no, (hop_no + 1) % how_many) for hop_no in range(how_many)],
+            )
+            so_far_all.append(main)
+        w2 = jnp.concatenate(so_far_all[::-1], axis=1)
+        high = lax.axis_index(group_axis)
+        return jnp.roll(w2, shift=(high + 1) * local_values.shape[1], axis=1)
+
+    gathered = guide_the_row(queries[0])
     query_count = gathered.shape[0]
     query_heads = gathered.reshape(query_count, kv_heads, -1, HEAD_DIM)
     moved_ids = move_page[0]

time: 191 us -> 260 us (1.36)
  waiting for transfers between devices: 87.8 us -> 153 us
  local copies, waits for them, and re-layouts: 14.7 us -> 30.6 us
  between operations: 15.6 us -> 2.64 us
    ppermute x0 -> x15, waiting for transfers between devices: none -> 106 us  [guide_the_row(): lax.ppermute(so_far_all[-1], group_axis, perm=[(hop_no, (hop_no + 1) % ho...]
    all_gather x1 -> x0, waiting for transfers between devices: 15 us -> none  [local(): gathered = lax.all_gather(queries[0], 'aa', axis=1, tiled=True)]
    unnamed x19 -> x86, local copies, waits for them, and re-layouts: 4.82 us -> 18.6 us
    all_to_all x1, waiting for transfers between devices: 13.6 us -> 0.01 us  [in_one_piece(): lax.all_to_all(both, axis, split_axis=split_dim, concat_axis=concat_dim,...]
    all_to_all x1, waiting for transfers between devices: 59.2 us -> 47.2 us  [sum_at_owner(): lax.all_to_all(split_up(value, dim, length), axis, 0, 0, tiled=True)]
  transfers between devices with their start and end apart: 4 -> 18, of which waited for: 3 -> 16; matrix products, arithmetic and copies ran while one was open for 15% -> 12% of each run, Pallas kernels for 0% -> 0%
where the time goes in v1:
time: 260 us; the launch traced here: 259 us
  waiting for transfers between devices  153 us (59%)
  matrix products  31.9 us (12%)
  local copies, waits for them, and re-layouts  30.6 us (12%)
  other arithmetic  22.4 us (9%)
  starting transfers between devices  18 us (7%)
  between operations  2.64 us (1%)
    ppermute x15, waiting for transfers between devices, guide_the_row(): lax.ppermute(so_far_all[-1], group_axis, perm=[(hop_no, (hop_no + 1) % ho...  106 us
    all_to_all x1, waiting for transfers between devices, sum_at_owner(): lax.all_to_all(split_up(value, dim, length), axis, 0, 0, tiled=True)  47.2 us
    dot_general x2, matrix products, block_step(): jnp.einsum('qkgr,rkd->qkgd', weights, block_values, precision=lax.Precisi...  21.1 us
    unnamed x86, local copies, waits for them, and re-layouts  18.6 us
    dot_general x2, matrix products, block_step(): jnp.einsum('qkgd,rkd->qkgr', query_heads, block_keys[:, 0], preferred_ele...  10.2 us
    reduce_sum x2, other arithmetic, block_step(): new_sum = run_sum * shrink + jnp.sum(weights, axis=-1)  9.9 us
    all_to_all x1, starting transfers between devices, sum_at_owner(): lax.all_to_all(split_up(value, dim, length), axis, 0, 0, tiled=True)  7.12 us
    all_to_all x1, starting transfers between devices, in_one_piece(): lax.all_to_all(both, axis, split_axis=split_dim, concat_axis=concat_dim,...  5.32 us
  transfers between devices with their start and end apart: 18, of which 16 were waited for; matrix products, arithmetic and copies ran while one was open for 12% of the time, Pallas kernels for 0%

profile of v1, /device:TPU:0, one launch (start us, length us, event | category | flops | bytes accessed | tf_op | source)
XLA Modules:
  0.0 258.8 jit_solution(14975823950791445954)
XLA Ops:
  0.6 1.1 copy.204
  1.8 1.1 copy.132
  2.9 1.6 collective-permute-start
  4.6 7.2 %collective-permute-done = bf16[128,512]{0,1:T(8,128)(2,1)S(1)} collective-permute-done((bf16[128,512]{0,1:T(8,128)(2,1)S(1)}, bf16[128,512]{0,1:T(8,128)(2,1)S(1)}, u32[]{:S(2)}, u32[]{:S(2)}) %collective-permute-start) | collective-permute-done | bytes 131104 | tf_op jit(solution)/shard_map/ppermute | solution.py:128
  11.8 0.7 fusion.44
  12.4 7.6 %collective-permute-done.1 = bf16[128,512]{0,1:T(8,128)(2,1)S(1)} collective-permute-done((bf16[128,512]{0,1:T(8,128)(2,1)S(1)}, bf16[128,512]{0,1:T(8,128)(2,1)S(1)}, u32[]{:S(2)}, u32[]{:S(2)}) %collective-permute-start.1) | collective-permute-done | bytes 131104 | tf_op jit(solution)/shard_map/ppermute | solution.py:128
  20.1 0.7 fusion.45
  20.7 7.6 %collective-permute-done.2 = bf16[128,512]{0,1:T(8,128)(2,1)S(1)} collective-permute-done((bf16[128,512]{0,1:T(8,128)(2,1)S(1)}, bf16[128,512]{0,1:T(8,128)(2,1)S(1)}, u32[]{:S(2)}, u32[]{:S(2)}) %collective-permute-start.2) | collective-permute-done | bytes 131104 | tf_op jit(solution)/shard_map/ppermute | solution.py:128
  28.4 1.5 gather_fusion.1
  30.2 0.9 convert_reduce_fusion
  31.1 5.6 %collective-permute-done.3 = bf16[128,512]{0,1:T(8,128)(2,1)S(1)} collective-permute-done((bf16[128,512]{0,1:T(8,128)(2,1)S(1)}, bf16[128,512]{0,1:T(8,128)(2,1)S(1)}, u32[]{:S(2)}, u32[]{:S(2)}) %collective-permute-start.3) | collective-permute-done | bytes 131104 | tf_op jit(solution)/shard_map/ppermute | solution.py:128
  36.6 0.7 fusion.46
  37.3 7.6 %collective-permute-done.4 = bf16[128,512]{0,1:T(8,128)(2,1)S(1)} collective-permute-done((bf16[128,512]{0,1:T(8,128)(2,1)S(1)}, bf16[128,512]{0,1:T(8,128)(2,1)S(1)}, u32[]{:S(2)}, u32[]{:S(2)}) %collective-permute-start.4) | collective-permute-done | bytes 131104 | tf_op jit(solution)/shard_map/ppermute | solution.py:128
  44.9 0.7 compare_and_fusion
  45.6 8.0 %collective-permute-done.5 = bf16[128,512]{0,1:T(8,128)(2,1)} collective-permute-done((bf16[128,512]{0,1:T(8,128)(2,1)S(1)}, bf16[128,512]{0,1:T(8,128)(2,1)}, u32[]{:S(2)}, u32[]{:S(2)}) %collective-permute-start.5) | collective-permute-done | bytes 131104 | tf_op jit(solution)/shard_map/ppermute | solution.py:128
  54.4 0.7 reshape_reshape.7
  55.1 8.5 %collective-permute-done.6 = bf16[128,512]{0,1:T(8,128)(2,1)} collective-permute-done((bf16[128,512]{0,1:T(8,128)(2,1)}, bf16[128,512]{0,1:T(8,128)(2,1)}, u32[]{:S(2)}, u32[]{:S(2)}) %collective-permute-start.6) | collective-permute-done | bytes 131104 | tf_op jit(solution)/shard_map/ppermute | solution.py:128
  63.6 1.9 pad_maximum_fusion
  65.5 5.3 %all-to-all-start = ((bf16[8,2,32769]{2,1,0:T(2,128)(2,1)}), bf16[8,2,32769]{2,1,0:T(2,128)(2,1)S(1)}, u32[]{:S(2)}, u32[]{:S(2)}) async-start(bf16[8,2,32769]{2,1,0:T(2,128)(2,1)} %pad_maximum_fusion), calls=%async_computation | async-start | bytes 2105344 | tf_op jit(solution)/shard_map/all_to_all | solution.py:17
  70.9 1.2 collective-permute-done.7
  73.0 1.1 gather_fusion
  74.2 6.2 %collective-permute-done.8 = bf16[128,512]{0,1:T(8,128)(2,1)S(1)} collective-permute-done((bf16[128,512]{0,1:T(8,128)(2,1)S(1)}, bf16[128,512]{0,1:T(8,128)(2,1)S(1)}, u32[]{:S(2)}, u32[]{:S(2)}) %collective-permute-start.8) | collective-permute-done | bytes 131104 | tf_op jit(solution)/shard_map/ppermute | solution.py:128
  80.6 8.2 %collective-permute-done.9 = bf16[128,512]{0,1:T(8,128)(2,1)S(1)} collective-permute-done((bf16[128,512]{0,1:T(8,128)(2,1)S(1)}, bf16[128,512]{0,1:T(8,128)(2,1)S(1)}, u32[]{:S(2)}, u32[]{:S(2)}) %collective-permute-start.9) | collective-permute-done | bytes 131104 | tf_op jit(solution)/shard_map/ppermute | solution.py:128
  88.8 0.8 reshape.296
  89.5 0.6 copy.131
  90.2 6.9 %collective-permute-done.10 = bf16[128,512]{0,1:T(8,128)(2,1)S(1)} collective-permute-done((bf16[128,512]{0,1:T(8,128)(2,1)S(1)}, bf16[128,512]{0,1:T(8,128)(2,1)S(1)}, u32[]{:S(2)}, u32[]{:S(2)}) %collective-permute-start.10) | collective-permute-done | bytes 131104 | tf_op jit(solution)/shard_map/ppermute | solution.py:128
  97.1 8.3 %collective-permute-done.11 = bf16[128,512]{0,1:T(8,128)(2,1)} collective-permute-done((bf16[128,512]{0,1:T(8,128)(2,1)S(1)}, bf16[128,512]{0,1:T(8,128)(2,1)}, u32[]{:S(2)}, u32[]{:S(2)}) %collective-permute-start.11) | collective-permute-done | bytes 131104 | tf_op jit(solution)/shard_map/ppermute | solution.py:128
  105.4 0.7 pad_add_fusion
  106.2 0.7 split.17
  106.9 0.8 squeeze.63
  107.7 6.3 %collective-permute-done.12 = bf16[128,512]{0,1:T(8,128)(2,1)} collective-permute-done((bf16[128,512]{0,1:T(8,128)(2,1)}, bf16[128,512]{0,1:T(8,128)(2,1)}, u32[]{:S(2)}, u32[]{:S(2)}) %collective-permute-start.12) | collective-permute-done | bytes 131104 | tf_op jit(solution)/shard_map/ppermute | solution.py:128
  114.9 8.5 %collective-permute-done.13 = bf16[128,512]{0,1:T(8,128)(2,1)} collective-permute-done((bf16[128,512]{0,1:T(8,128)(2,1)}, bf16[128,512]{0,1:T(8,128)(2,1)}, u32[]{:S(2)}, u32[]{:S(2)}) %collective-permute-start.13) | collective-permute-done | bytes 131104 | tf_op jit(solution)/shard_map/ppermute | solution.py:128
  123.8 8.2 %collective-permute-done.14 = bf16[128,512]{0,1:T(8,128)(2,1)S(1)} collective-permute-done((bf16[128,512]{0,1:T(8,128)(2,1)}, bf16[128,512]{0,1:T(8,128)(2,1)S(1)}, u32[]{:S(2)}, u32[]{:S(2)}) %collective-permute-start.14) | collective-permute-done | bytes 131104 | tf_op jit(solution)/shard_map/ppermute | solution.py:128
  132.0 0.9 constant_dynamic-update-slice_fusion.30
  132.9 0.9 constant_dynamic-update-slice_fusion.29
  133.8 0.9 constant_dynamic-update-slice_fusion.28
  134.8 0.9 constant_dynamic-update-slice_fusion.27
  135.7 0.9 constant_dynamic-update-slice_fusion.26
  136.6 0.9 constant_dynamic-update-slice_fusion.25
  137.5 0.9 constant_dynamic-update-slice_fusion.24
  138.5 0.9 constant_dynamic-update-slice_fusion.23
  139.4 0.9 constant_dynamic-update-slice_fusion.22
  140.3 0.9 constant_dynamic-update-slice_fusion.21
  141.3 0.9 constant_dynamic-update-slice_fusion.20
  142.3 0.9 constant_dynamic-update-slice_fusion.14
  143.3 0.9 constant_dynamic-update-slice_fusion.13
  144.2 0.9 constant_dynamic-update-slice_fusion.12
  145.3 0.9 constant_dynamic-update-slice_fusion.7
  146.2 0.9 constant_dynamic-update-slice_fusion.6
  147.5 7.3 %bitcast_reduce_fusion = (f32[128,4,16]{0,2,1:T(8,128)S(1)}, f32[4,512,128,16]{2,1,3,0:T(8,128)}) fusion(pred[512]{0:T(512)(128)(4,1)S(1)} %broadcast_in_dim.133, bf16[128,4,16,128]{0,3,2,1:T(8,128)(2,1)S(1)} %bitcast.114, bf16[512,1,4,128]{3,2,1,0:T(4,128)(2,1)S(1)} %get-tuple-element.59), kind=kOutput, calls=%fused_computation.4 | convolution fusion | flops 1086316544 | bytes 19431936 | tf_op jit(solution)/shard_map/while/body/eval_jaxpr/qkgd,rkd->qkgr/dot_general | solution.py:89
  154.8 2.9 %fusion.15 = (f32[128,4,16]{0,2,1:T(8,128)S(1)}, f32[4,136,128,16]{2,1,3,0:T(8,128)}) fusion(pred[128,136]{0,1:T(8,128)(4,1)S(1)} %copy-done.19, bf16[128,4,16,128]{0,3,2,1:T(8,128)(2,1)S(1)} %bitcast.115, bf16[128,2,4,128]{3,0,2,1:T(8,128)(2,1)S(1)} %copy_select_fusion, bf16[8,2,4,128]{3,0,2,1:T(8,128)(2,1)S(1)} %copy-done.20), kind=kOutput, calls=%fused_computation.25 | convolution fusion | flops 288825344 | bytes 6882304 | tf_op jit(solution)/shard_map/while/body/eval_jaxpr/qkgd,rkd->qkgr/dot_general | solution.py:89
  157.7 0.9 broadcast_in_dim.138
  158.5 3.9 %all-to-all-start.1 = ((f32[16,128,4,16]{1,3,2,0:T(8,128)}), f32[16,128,4,16]{1,3,2,0:T(8,128)S(1)}, u32[]{:S(2)}, u32[]{:S(2)}) async-start(f32[16,128,4,16]{1,3,2,0:T(8,128)} %broadcast_in_dim.138), calls=%async_computation.1 | async-start | bytes 1048576 | tf_op jit(solution)/shard_map/all_to_all | solution.py:26
  162.5 8.6 %fusion.2 = f32[128,4,16]{0,2,1:T(8,128)S(1)} fusion(f32[4,512,128,16]{2,1,3,0:T(8,128)} %get-tuple-element.69, f32[128,4,16]{0,2,1:T(8,128)S(1)} %get-tuple-element.62, pred[512]{0:T(512)(128)(4,1)S(1)} %broadcast_in_dim.133), kind=kLoop, calls=%fused_computation.8 | loop fusion | flops 20963328 | bytes 16843264 | tf_op jit(solution)/shard_map/while/body/eval_jaxpr/reduce_sum | solution.py:99
  171.1 1.3 fusion.16
  172.4 5.3 %fusion.17 = f32[4,128,128,16]{2,1,3,0:T(8,128)} fusion(f32[4,136,128,16]{2,1,3,0:T(8,128)S(1)} %bitcast.113, f32[128,4,16]{0,2,1:T(8,128)S(1)} %get-tuple-element.65, pred[128,136]{0,1:T(8,128)(4,1)S(1)} %copy-done.19, bf16[8,2,4,128]{3,0,2,1:T(8,128)(2,1)S(1)} %copy-done.20, bf16[128,2,4,128]{3,0,2,1:T(8,128)(2,1)S(1)} %copy_select_fusion), kind=kOutput, calls=%fused_computation.27 | convolution fusion | flops 1716011008 | bytes 8979456 | tf_op jit(solution)/shard_map/while/body/eval_jaxpr/qkgr,rkd->qkgd/dot_general | solution.py:101
  177.8 15.8 %fusion.13 = f32[128,4,16,128]{0,3,2,1:T(8,128)S(1)} fusion(f32[4,128,128,16]{2,1,3,0:T(8,128)} %fusion.17, f32[4,512,128,16]{2,1,3,0:T(8,128)} %get-tuple-element.69, f32[128,4,16]{0,2,1:T(8,128)S(1)} %get-tuple-element.62, pred[512]{0:T(512)(128)(4,1)S(1)} %broadcast_in_dim.133, f32[128,4,16]{0,2,1:T(8,128)S(1)} %get-tuple-element.64, ...), kind=kOutput, calls=%fused_computation.22 | convolution fusion | flops 6465519616 | bytes 25887232 | tf_op jit(solution)/shard_map/while/body/eval_jaxpr/qkgr,rkd->qkgd/dot_general | solution.py:101
  193.6 2.8 %copy.141 = f32[128,16,4,128]{0,2,3,1:T(4,128)S(1)} copy(f32[128,16,4,128]{0,3,2,1:T(8,128)S(1)} %bitcast.116) | data formatting | bytes 8388608 | tf_op jit(solution)/shard_map/concatenate | solution.py:49
  196.5 3.0 %maximum_bitcast_fusion = f32[16,128,4,129]{1,2,3,0:T(4,128)} fusion(f32[128,16,4,1]{0,2,3,1:T(4,128)S(1)} %exponential_multiply_fusion, f32[128,16,4,128]{0,2,3,1:T(4,128)S(1)} %copy.141), kind=kLoop, calls=%fused_computation.18 | loop fusion | flops 1056768 | bytes 8454144 | tf_op jit(solution)/shard_map/transpose | solution.py:38
  199.5 7.1 %all-to-all-start.2 = ((f32[16,128,4,129]{1,2,3,0:T(4,128)}), f32[16,128,4,129]{1,2,3,0:T(4,128)}, u32[]{:S(2)}, u32[]{:S(2)}) async-start(f32[16,128,4,129]{1,2,3,0:T(4,128)} %maximum_bitcast_fusion), calls=%async_computation.2 | async-start | bytes 8454144 | tf_op jit(solution)/shard_map/all_to_all | solution.py:43
  207.3 0.6 bitcast_dynamic-update-slice_fusion
  207.9 47.2 %all-to-all-done.2 = f32[16,128,4,129]{1,2,3,0:T(4,128)} async-done(((f32[16,128,4,129]{1,2,3,0:T(4,128)}), f32[16,128,4,129]{1,2,3,0:T(4,128)}, u32[]{:S(2)}, u32[]{:S(2)}) %all-to-all-start.2) | async-done | bytes 4227104 | tf_op jit(solution)/shard_map/all_to_all | solution.py:43
  255.1 2.9 %reduce_sum.63 = f32[128,4,129]{0,1,2:T(4,128)S(1)} reduce(f32[16,128,4,129]{1,2,3,0:T(4,128)} %all-to-all-done.2, f32[]{:T(128)} %constant.71.clone.1), dimensions={0}, to_apply=%region_7.8 | reduce | flops 990720 | bytes 4491268 | tf_op jit(solution)/shard_map/reduce_sum | solution.py:44
  258.0 0.8 copy.143
  (113 shorter events, 3.4 us)
Async XLA Ops:
  1.8 71.2 %copy-start = (bf16[1,12,32,2,512]{4,3,2,1,0:T(2,128)(2,1)}, bf16[1,12,32,2,512]{4,3,2,1,0:T(2,128)(2,1)S(1)}, u32[]{:S(2)}) copy-start(bf16[1,12,32,2,512]{4,3,2,1,0:T(2,128)(2,1)S(1)} %copy.204) | copy-start | bytes 2359300
  2.9 8.9 %collective-permute-start = (bf16[128,512]{0,1:T(8,128)(2,1)S(1)}, bf16[128,512]{0,1:T(8,128)(2,1)S(1)}, u32[]{:S(2)}, u32[]{:S(2)}) collective-permute-start(bf16[128,512]{0,1:T(8,128)(2,1)S(1)} %bitcast.119), channel_id=1, source_target_pairs={{0,8},{8,16},{16,24},{24,32},{32,40},{40,48},{48,56},{56,64},{64,7... | collective-permute-start | bytes 393224 | tf_op jit(solution)/shard_map/ppermute | solution.py:128
  11.8 53.8 %copy-start.1 = (bf16[128,512]{0,1:T(8,128)(2,1)}, bf16[128,512]{0,1:T(8,128)(2,1)S(1)}, u32[]{:S(2)}) copy-start(bf16[128,512]{0,1:T(8,128)(2,1)S(1)} %collective-permute-done) | copy-start | bytes 393220
  11.8 8.3 %collective-permute-start.1 = (bf16[128,512]{0,1:T(8,128)(2,1)S(1)}, bf16[128,512]{0,1:T(8,128)(2,1)S(1)}, u32[]{:S(2)}, u32[]{:S(2)}) collective-permute-start(bf16[128,512]{0,1:T(8,128)(2,1)S(1)} %collective-permute-done), channel_id=1, source_target_pairs={{0,8},{8,16},{16,24},{24,32},{32,40},{40,48},{48,56},{56,64},{64,7... | collective-permute-start | bytes 393224 | tf_op jit(solution)/shard_map/ppermute | solution.py:128
  20.1 45.5 %copy-start.3 = (bf16[128,512]{0,1:T(8,128)(2,1)}, bf16[128,512]{0,1:T(8,128)(2,1)S(1)}, u32[]{:S(2)}) copy-start(bf16[128,512]{0,1:T(8,128)(2,1)S(1)} %collective-permute-done.1) | copy-start | bytes 393220
  20.1 8.3 %collective-permute-start.2 = (bf16[128,512]{0,1:T(8,128)(2,1)S(1)}, bf16[128,512]{0,1:T(8,128)(2,1)S(1)}, u32[]{:S(2)}, u32[]{:S(2)}) collective-permute-start(bf16[128,512]{0,1:T(8,128)(2,1)S(1)} %collective-permute-done.1), channel_id=1, source_target_pairs={{0,8},{8,16},{16,24},{24,32},{32,40},{40,48},{48,56},{56,64},{64,7... | collective-permute-start | bytes 393224 | tf_op jit(solution)/shard_map/ppermute | solution.py:128
  28.4 37.2 %copy-start.5 = (bf16[128,512]{0,1:T(8,128)(2,1)}, bf16[128,512]{0,1:T(8,128)(2,1)S(1)}, u32[]{:S(2)}) copy-start(bf16[128,512]{0,1:T(8,128)(2,1)S(1)} %collective-permute-done.2) | copy-start | bytes 393220
  28.4 8.3 %collective-permute-start.3 = (bf16[128,512]{0,1:T(8,128)(2,1)S(1)}, bf16[128,512]{0,1:T(8,128)(2,1)S(1)}, u32[]{:S(2)}, u32[]{:S(2)}) collective-permute-start(bf16[128,512]{0,1:T(8,128)(2,1)S(1)} %collective-permute-done.2), channel_id=1, source_target_pairs={{0,8},{8,16},{16,24},{24,32},{32,40},{40,48},{48,56},{56,64},{64,7... | collective-permute-start | bytes 393224 | tf_op jit(solution)/shard_map/ppermute | solution.py:128
  29.8 42.3 %copy-start.22 = (s32[1,4]{1,0:T(1,128)S(1)}, s32[1,4]{1,0:T(1,128)}, u32[]{:S(2)}) copy-start(s32[1,4]{1,0:T(1,128)} %param.11) | copy-start | bytes 52
  36.6 43.8 %copy-start.7 = (bf16[128,512]{0,1:T(8,128)(2,1)}, bf16[128,512]{0,1:T(8,128)(2,1)S(1)}, u32[]{:S(2)}) copy-start(bf16[128,512]{0,1:T(8,128)(2,1)S(1)} %collective-permute-done.3) | copy-start | bytes 393220
  36.6 8.3 %collective-permute-start.4 = (bf16[128,512]{0,1:T(8,128)(2,1)S(1)}, bf16[128,512]{0,1:T(8,128)(2,1)S(1)}, u32[]{:S(2)}, u32[]{:S(2)}) collective-permute-start(bf16[128,512]{0,1:T(8,128)(2,1)S(1)} %collective-permute-done.3), channel_id=1, source_target_pairs={{0,8},{8,16},{16,24},{24,32},{32,40},{40,48},{48,56},{56,64},{64,7... | collective-permute-start | bytes 393224 | tf_op jit(solution)/shard_map/ppermute | solution.py:128
  44.9 9.4 %copy-start.9 = (bf16[128,512]{0,1:T(8,128)(2,1)}, bf16[128,512]{0,1:T(8,128)(2,1)S(1)}, u32[]{:S(2)}) copy-start(bf16[128,512]{0,1:T(8,128)(2,1)S(1)} %collective-permute-done.4) | copy-start | bytes 393220
  44.9 8.7 %collective-permute-start.5 = (bf16[128,512]{0,1:T(8,128)(2,1)S(1)}, bf16[128,512]{0,1:T(8,128)(2,1)}, u32[]{:S(2)}, u32[]{:S(2)}) collective-permute-start(bf16[128,512]{0,1:T(8,128)(2,1)S(1)} %collective-permute-done.4), channel_id=1, source_target_pairs={{0,8},{8,16},{16,24},{24,32},{32,40},{40,48},{48,56},{56,64},{64,7... | collective-permute-start | bytes 393224 | tf_op jit(solution)/shard_map/ppermute | solution.py:128
  53.6 10.0 %collective-permute-start.6 = (bf16[128,512]{0,1:T(8,128)(2,1)}, bf16[128,512]{0,1:T(8,128)(2,1)}, u32[]{:S(2)}, u32[]{:S(2)}) collective-permute-start(bf16[128,512]{0,1:T(8,128)(2,1)} %collective-permute-done.5), channel_id=1, source_target_pairs={{0,8},{8,16},{16,24},{24,32},{32,40},{40,48},{48,56},{56,64},{64,7... | collective-permute-start | bytes 393224 | tf_op jit(solution)/shard_map/ppermute | solution.py:128
  63.6 8.5 %collective-permute-start.7 = (bf16[128,512]{0,1:T(8,128)(2,1)}, bf16[128,512]{0,1:T(8,128)(2,1)S(1)}, u32[]{:S(2)}, u32[]{:S(2)}) collective-permute-start(bf16[128,512]{0,1:T(8,128)(2,1)} %collective-permute-done.6), channel_id=1, source_target_pairs={{0,8},{8,16},{16,24},{24,32},{32,40},{40,48},{48,56},{56,64},{64,7... | collective-permute-start | bytes 393224 | tf_op jit(solution)/shard_map/ppermute | solution.py:128
  65.5 40.6 %all-to-all-start = ((bf16[8,2,32769]{2,1,0:T(2,128)(2,1)}), bf16[8,2,32769]{2,1,0:T(2,128)(2,1)S(1)}, u32[]{:S(2)}, u32[]{:S(2)}) async-start(bf16[8,2,32769]{2,1,0:T(2,128)(2,1)} %pad_maximum_fusion), calls=%async_computation | async-start | bytes 2105344 | tf_op jit(solution)/shard_map/all_to_all | solution.py:17
  72.1 34.0 %copy-start.11 = (bf16[128,512]{0,1:T(8,128)(2,1)}, bf16[128,512]{0,1:T(8,128)(2,1)S(1)}, u32[]{:S(2)}) copy-start(bf16[128,512]{0,1:T(8,128)(2,1)S(1)} %collective-permute-done.7) | copy-start | bytes 393220
  72.1 8.4 %collective-permute-start.8 = (bf16[128,512]{0,1:T(8,128)(2,1)S(1)}, bf16[128,512]{0,1:T(8,128)(2,1)S(1)}, u32[]{:S(2)}, u32[]{:S(2)}) collective-permute-start(bf16[128,512]{0,1:T(8,128)(2,1)S(1)} %collective-permute-done.7), channel_id=1, source_target_pairs={{0,8},{8,16},{16,24},{24,32},{32,40},{40,48},{48,56},{56,64},{64,7... | collective-permute-start | bytes 393224 | tf_op jit(solution)/shard_map/ppermute | solution.py:128
  80.5 25.7 %copy-start.13 = (bf16[128,512]{0,1:T(8,128)(2,1)}, bf16[128,512]{0,1:T(8,128)(2,1)S(1)}, u32[]{:S(2)}) copy-start(bf16[128,512]{0,1:T(8,128)(2,1)S(1)} %collective-permute-done.8) | copy-start | bytes 393220
  80.5 8.3 %collective-permute-start.9 = (bf16[128,512]{0,1:T(8,128)(2,1)S(1)}, bf16[128,512]{0,1:T(8,128)(2,1)S(1)}, u32[]{:S(2)}, u32[]{:S(2)}) collective-permute-start(bf16[128,512]{0,1:T(8,128)(2,1)S(1)} %collective-permute-done.8), channel_id=1, source_target_pairs={{0,8},{8,16},{16,24},{24,32},{32,40},{40,48},{48,56},{56,64},{64,7... | collective-permute-start | bytes 393224 | tf_op jit(solution)/shard_map/ppermute | solution.py:128
  88.7 17.4 %copy-start.15 = (bf16[128,512]{0,1:T(8,128)(2,1)}, bf16[128,512]{0,1:T(8,128)(2,1)S(1)}, u32[]{:S(2)}) copy-start(bf16[128,512]{0,1:T(8,128)(2,1)S(1)} %collective-permute-done.9) | copy-start | bytes 393220
  88.7 8.3 %collective-permute-start.10 = (bf16[128,512]{0,1:T(8,128)(2,1)S(1)}, bf16[128,512]{0,1:T(8,128)(2,1)S(1)}, u32[]{:S(2)}, u32[]{:S(2)}) collective-permute-start(bf16[128,512]{0,1:T(8,128)(2,1)S(1)} %collective-permute-done.9), channel_id=1, source_target_pairs={{0,8},{8,16},{16,24},{24,32},{32,40},{40,48},{48,56},{56,64},{64,7... | collective-permute-start | bytes 393224 | tf_op jit(solution)/shard_map/ppermute | solution.py:128
  97.0 9.1 %copy-start.17 = (bf16[128,512]{0,1:T(8,128)(2,1)}, bf16[128,512]{0,1:T(8,128)(2,1)S(1)}, u32[]{:S(2)}) copy-start(bf16[128,512]{0,1:T(8,128)(2,1)S(1)} %collective-permute-done.10) | copy-start | bytes 393220
  97.0 8.4 %collective-permute-start.11 = (bf16[128,512]{0,1:T(8,128)(2,1)S(1)}, bf16[128,512]{0,1:T(8,128)(2,1)}, u32[]{:S(2)}, u32[]{:S(2)}) collective-permute-start(bf16[128,512]{0,1:T(8,128)(2,1)S(1)} %collective-permute-done.10), channel_id=1, source_target_pairs={{0,8},{8,16},{16,24},{24,32},{32,40},{40,48},{48,56},{56,64},{64,7... | collective-permute-start | bytes 393224 | tf_op jit(solution)/shard_map/ppermute | solution.py:128
  105.4 8.6 %collective-permute-start.12 = (bf16[128,512]{0,1:T(8,128)(2,1)}, bf16[128,512]{0,1:T(8,128)(2,1)}, u32[]{:S(2)}, u32[]{:S(2)}) collective-permute-start(bf16[128,512]{0,1:T(8,128)(2,1)} %collective-permute-done.11), channel_id=1, source_target_pairs={{0,8},{8,16},{16,24},{24,32},{32,40},{40,48},{48,56},{56,64},{64,7... | collective-permute-start | bytes 393224 | tf_op jit(solution)/shard_map/ppermute | solution.py:128
  114.0 9.4 %collective-permute-start.13 = (bf16[128,512]{0,1:T(8,128)(2,1)}, bf16[128,512]{0,1:T(8,128)(2,1)}, u32[]{:S(2)}, u32[]{:S(2)}) collective-permute-start(bf16[128,512]{0,1:T(8,128)(2,1)} %collective-permute-done.12), channel_id=1, source_target_pairs={{0,8},{8,16},{16,24},{24,32},{32,40},{40,48},{48,56},{56,64},{64,7... | collective-permute-start | bytes 393224 | tf_op jit(solution)/shard_map/ppermute | solution.py:128
  114.4 27.8 %copy-start.6 = (bf16[128,512]{0,1:T(8,128)(2,1)S(1)}, bf16[128,512]{0,1:T(8,128)(2,1)}, u32[]{:S(2)}) copy-start(bf16[128,512]{0,1:T(8,128)(2,1)} %copy-done.5) | copy-start | bytes 393220
  114.4 27.8 %copy-start.4 = (bf16[128,512]{0,1:T(8,128)(2,1)S(1)}, bf16[128,512]{0,1:T(8,128)(2,1)}, u32[]{:S(2)}) copy-start(bf16[128,512]{0,1:T(8,128)(2,1)} %copy-done.3) | copy-start | bytes 393220
  114.4 27.8 %copy-start.2 = (bf16[128,512]{0,1:T(8,128)(2,1)S(1)}, bf16[128,512]{0,1:T(8,128)(2,1)}, u32[]{:S(2)}) copy-start(bf16[128,512]{0,1:T(8,128)(2,1)} %copy-done.1) | copy-start | bytes 393220
  114.4 32.7 %copy-start.10 = (bf16[128,512]{0,1:T(8,128)(2,1)S(1)}, bf16[128,512]{0,1:T(8,128)(2,1)}, u32[]{:S(2)}) copy-start(bf16[128,512]{0,1:T(8,128)(2,1)} %copy-done.9) | copy-start | bytes 393220
  114.4 32.7 %copy-start.8 = (bf16[128,512]{0,1:T(8,128)(2,1)S(1)}, bf16[128,512]{0,1:T(8,128)(2,1)}, u32[]{:S(2)}) copy-start(bf16[128,512]{0,1:T(8,128)(2,1)} %copy-done.7) | copy-start | bytes 393220
  114.5 30.7 %copy-start.18 = (bf16[128,512]{0,1:T(8,128)(2,1)S(1)}, bf16[128,512]{0,1:T(8,128)(2,1)}, u32[]{:S(2)}) copy-start(bf16[128,512]{0,1:T(8,128)(2,1)} %copy-done.17) | copy-start | bytes 393220
  114.5 30.7 %copy-start.16 = (bf16[128,512]{0,1:T(8,128)(2,1)S(1)}, bf16[128,512]{0,1:T(8,128)(2,1)}, u32[]{:S(2)}) copy-start(bf16[128,512]{0,1:T(8,128)(2,1)} %copy-done.15) | copy-start | bytes 393220
  114.5 30.7 %copy-start.14 = (bf16[128,512]{0,1:T(8,128)(2,1)S(1)}, bf16[128,512]{0,1:T(8,128)(2,1)}, u32[]{:S(2)}) copy-start(bf16[128,512]{0,1:T(8,128)(2,1)} %copy-done.13) | copy-start | bytes 393220
  114.5 30.7 %copy-start.12 = (bf16[128,512]{0,1:T(8,128)(2,1)S(1)}, bf16[128,512]{0,1:T(8,128)(2,1)}, u32[]{:S(2)}) copy-start(bf16[128,512]{0,1:T(8,128)(2,1)} %copy-done.11) | copy-start | bytes 393220
  123.5 8.5 %collective-permute-start.14 = (bf16[128,512]{0,1:T(8,128)(2,1)}, bf16[128,512]{0,1:T(8,128)(2,1)S(1)}, u32[]{:S(2)}, u32[]{:S(2)}) collective-permute-start(bf16[128,512]{0,1:T(8,128)(2,1)} %collective-permute-done.13), channel_id=1, source_target_pairs={{0,8},{8,16},{16,24},{24,32},{32,40},{40,48},{48,56},{56,64},{64,7... | collective-permute-start | bytes 393224 | tf_op jit(solution)/shard_map/ppermute | solution.py:128
  147.5 7.3 %copy-start.19 = (pred[128,136]{0,1:T(8,128)(4,1)S(1)}, pred[128,136]{0,1:T(8,128)(4,1)}, u32[]{:S(2)}) copy-start(pred[128,136]{0,1:T(8,128)(4,1)} %pad_add_fusion) | copy-start | bytes 52228
  147.5 7.3 %copy-start.20 = (bf16[8,2,4,128]{3,0,2,1:T(8,128)(2,1)S(1)}, bf16[8,2,4,128]{3,0,2,1:T(8,128)(2,1)}, u32[]{:S(2)}) copy-start(bf16[8,2,4,128]{3,0,2,1:T(8,128)(2,1)} %copy.131) | copy-start | bytes 49156
  158.5 12.6 %slice-start = ((s8[4456448]{0:T(1024)(128)(4,1)}), s8[262144]{0:T(1024)(128)(4,1)S(1)}, s32[]{:S(2)}) async-start(s8[4456448]{0:T(1024)(128)(4,1)} %bitcast.112), calls=%async_computation.3 | async-start | bytes 524288
  158.5 19.2 %all-to-all-start.1 = ((f32[16,128,4,16]{1,3,2,0:T(8,128)}), f32[16,128,4,16]{1,3,2,0:T(8,128)S(1)}, u32[]{:S(2)}, u32[]{:S(2)}) async-start(f32[16,128,4,16]{1,3,2,0:T(8,128)} %broadcast_in_dim.138), calls=%async_computation.1 | async-start | bytes 1048576 | tf_op jit(solution)/shard_map/all_to_all | solution.py:26
  162.5 8.6 %slice-start.1 = ((s8[4456448]{0:T(1024)(128)(4,1)}), s8[4194304]{0:T(1024)(128)(4,1)S(1)}, s32[]{:S(2)}) async-start(s8[4456448]{0:T(1024)(128)(4,1)} %bitcast.112), calls=%async_computation.4 | async-start | bytes 8388608
  199.5 7.8 %copy-start.21 = (bf16[1,8,2,512]{3,2,1,0:T(2,128)(2,1)S(1)}, bf16[1,8,2,512]{3,2,1,0:T(2,128)(2,1)}, u32[]{:S(2)}) copy-start(bf16[1,8,2,512]{3,2,1,0:T(2,128)(2,1)} %param.9) | copy-start | bytes 49156
  199.5 55.6 %all-to-all-start.2 = ((f32[16,128,4,129]{1,2,3,0:T(4,128)}), f32[16,128,4,129]{1,2,3,0:T(4,128)}, u32[]{:S(2)}, u32[]{:S(2)}) async-start(f32[16,128,4,129]{1,2,3,0:T(4,128)} %maximum_bitcast_fusion), calls=%async_computation.2 | async-start | bytes 8454144 | tf_op jit(solution)/shard_map/all_to_all | solution.py:43
